TPU v7x, 32 devices: a whole 2x2x4 slice. The times are simulated.
32 devices in a mesh: dp: 2 (over y), fsdp: 4 (over z), tensor: 4 (over x, core).
Axes of the slice: x: 2, y: 2, z: 4, core: 2. Of those that a mesh axis runs over, the one named last changes fastest.
Arguments:
- weight: float32 [4096, 4096], P('fsdp', 'tensor'), may hold values from -0.000234375 to 0.000234375
- momentum: bfloat16 [2, 4096, 4096], P('dp', 'fsdp', 'tensor'), may hold values from -8 to 8
- grads: bfloat16 [2, 2, 4096, 4096], P('dp', None, 'fsdp', 'tensor'), may hold values from -8 to 8
- right_factor: float32 [64, 4096], P(None, 'tensor'), may hold values from -1 to 1
Outputs:
- new_weight: float32 [4096, 4096], P('fsdp', 'tensor')
- new_momentum: bfloat16 [2, 4096, 4096], P('dp', 'fsdp', 'tensor')
- new_right: float32 [64, 4096], P(None, 'tensor')
All inputs are finite; a program needn't handle non-finite values.
Results may differ from a plain program's by a relative error of at most 0.001.
Values sent between devices are 32-bit elements; how exact they have to be, the bound alone decides.
No kernel may reach another device: no remote copies, remote signals or barrier semaphores. Data moves between devices by JAX's collectives and lax.ppermute only.
A program may use at most 64 MiB of HBM per device.

v0:
```python
import math
import jax
import jax.numpy as jnp
from jax import lax
from jax.sharding import PartitionSpec as P

ROWS = 4096
COLS = 4096
decay_part = 0.05
learn_rate = 0.02
epsilon = 1e-06


def cholesky_step(factor, gram):
    lower = jnp.linalg.cholesky(gram)
    return jax.scipy.linalg.solve_triangular(lower, factor.T, lower=True).T


def local_gram(factor):
    return jnp.dot(
        factor.T, factor, precision=lax.Precision.HIGHEST, preferred_element_type=jnp.float32
    )


def orthonormal_rows(factor):
    for sweep in range(2):
        gram = lax.psum(local_gram(factor), "fsdp")
        factor = cholesky_step(factor, gram)
    return factor


def normalize(shared, sums):
    return shared / jnp.sqrt(sums + epsilon)[:, None]


def local(weight, momentum, grads, right_factor):
    replicas = lax.axis_size("dp")
    blended = momentum[0].astype(jnp.float32) + jnp.sum(grads[0].astype(jnp.float32), axis=0)
    partial_value = (
        jnp.dot(
            blended,
            right_factor.T,
            precision=lax.Precision.HIGHEST,
            preferred_element_type=jnp.float32,
        )
        / replicas
    )
    left = orthonormal_rows(lax.psum(partial_value, ("dp", "tensor")))
    partial_right = lax.dot_general(
        left,
        blended,
        (((0,), (0,)), ((), ())),
        precision=lax.Precision.HIGHEST,
        preferred_element_type=jnp.float32,
    )
    replica_right = lax.psum(partial_right, "fsdp")
    shared = lax.psum(replica_right, "dp") / replicas
    sums = lax.psum(jnp.sum(shared * shared, axis=1), "tensor")
    new_right = normalize(shared, sums)
    projected = jnp.dot(
        left, replica_right, precision=lax.Precision.HIGHEST, preferred_element_type=jnp.float32
    )
    new_momentum = (blended - decay_part * projected).astype(jnp.bfloat16)[None]
    scale = learn_rate * math.sqrt(ROWS / COLS)
    new_weight = weight - scale * jnp.dot(
        left, new_right, precision=lax.Precision.HIGHEST, preferred_element_type=jnp.float32
    )
    return (new_weight, new_momentum, new_right)


def solution(mesh):
    placed = (
        P("fsdp", "tensor"),
        P("dp", "fsdp", "tensor"),
        P("dp", None, "fsdp", "tensor"),
        P(None, "tensor"),
    )
    return jax.shard_map(
        local,
        mesh=mesh,
        in_specs=placed,
        out_specs=(P("fsdp", "tensor"), P("dp", "fsdp", "tensor"), P(None, "tensor")),
        check_vma=False,
    )
```

profile of v0, /device:TPU:0, one launch (start us, length us, event | category | flops | bytes accessed | tf_op | source)
XLA Modules:
  0.0 231.3 jit_solution(12908039776124173069)
XLA Ops:
  7.2 4.0 %convert_reduce_fusion = f32[1024,1024]{1,0:T(8,128)S(1)} fusion(bf16[1,2,1024,1024]{3,2,1,0:T(8,128)(2,1)} %param.9), kind=kLoop, calls=%fused_computation | loop fusion | flops 3145728 | bytes 8388608 | tf_op jit(solution)/shard_map/reduce_sum | solution.py:38
  11.2 2.0 copy-done.1
  13.2 5.1 %fusion.3 = f32[1024,64]{0,1:T(8,128)} fusion(f32[64,1024]{1,0:T(8,128)S(1)} %copy-done, f32[1024,1024]{1,0:T(8,128)S(1)} %convert_reduce_fusion, bf16[1,1024,1024]{2,1,0:T(8,128)(2,1)S(1)} %copy-done.2), kind=kOutput, calls=%fused_computation.7 | convolution fusion | flops 807469056 | bytes 6815744 | tf_op jit(solution)/shard_map/dot_general | solution.py:40
  18.4 56.7 %all-reduce.4.cloned.1.call-done = f32[1024,64]{0,1:T(8,128)} async-done(((f32[1024,64]{0,1:T(8,128)}), f32[1024,64]{0,1:T(8,128)}) %all-reduce.4.cloned.1.call-update) | async-done | bytes 262160 | tf_op jit(solution)/shard_map/psum | solution.py:48
  75.1 1.4 fusion.15
  76.5 19.0 %psum.43 = f32[64,64]{0,1:T(8,128)S(1)} all-reduce(f32[64,64]{0,1:T(8,128)S(1)} %fusion.15), channel_id=1, replica_groups=mesh['dp'=2,'fsdp'=4,'tensor'=4] {'fsdp'}, use_global_device_ids=true, to_apply=%region_2.0 | all-reduce | flops 4096 | bytes 32768 | tf_op jit(solution)/shard_map/psum | solution.py:27
  95.6 5.8 %cholesky.44 = f32[64,64]{1,0:T(8,128)S(1)} custom-call(f32[64,64]{1,0:T(8,128)S(1)} %fusion.12), custom_call_target="Cholesky" | custom-call | tf_op jit(solution)/shard_map/jit(cholesky)/cholesky | solution.py:15
  101.4 0.6 compare_reduce_fusion.1
  102.1 0.7 fusion.6
  102.8 4.9 %custom-call.6 = f32[1,64,64]{1,2,0:T(8,128)S(1)} custom-call(f32[1,64,64]{2,1,0:T(8,128)S(1)} %fusion.6), custom_call_target="InvertDiagBlocksLowerTriangular" | custom-call | tf_op jit(solution)/shard_map/jit(_solve_triangular)/triangular_solve | solution.py:16
  107.6 1.4 fusion.4
  109.4 16.1 %psum.44 = f32[64,64]{0,1:T(8,128)S(1)} all-reduce(f32[64,64]{0,1:T(8,128)S(1)} %fusion.16), channel_id=1, replica_groups=mesh['dp'=2,'fsdp'=4,'tensor'=4] {'fsdp'}, use_global_device_ids=true, to_apply=%region_5.0 | all-reduce | flops 4096 | bytes 32768 | tf_op jit(solution)/shard_map/psum | solution.py:27
  125.6 5.8 %cholesky.55 = f32[64,64]{1,0:T(8,128)S(1)} custom-call(f32[64,64]{1,0:T(8,128)S(1)} %fusion.10), custom_call_target="Cholesky" | custom-call | tf_op jit(solution)/shard_map/jit(cholesky)/cholesky | solution.py:15
  132.2 0.7 fusion.7
  132.8 4.9 %custom-call.7 = f32[1,64,64]{1,2,0:T(8,128)S(1)} custom-call(f32[1,64,64]{2,1,0:T(8,128)S(1)} %fusion.7), custom_call_target="InvertDiagBlocksLowerTriangular" | custom-call | tf_op jit(solution)/shard_map/jit(_solve_triangular)/triangular_solve | solution.py:16
  138.2 5.7 %fusion.1 = f32[64,1024]{1,0:T(8,128)} fusion(f32[64,1024]{1,0:T(8,128)S(1)} %fusion.8, f32[1024,1024]{1,0:T(8,128)} %copy-done.1, bf16[1,1024,1024]{2,1,0:T(8,128)(2,1)S(1)} %copy-done.2), kind=kOutput, calls=%fused_computation.5 | convolution fusion | flops 807403520 | bytes 6815744 | tf_op jit(solution)/shard_map/dot_general | solution.py:49
  143.9 33.2 %all-reduce.6.cloned.1.call-done = f32[64,1024]{1,0:T(8,128)} async-done(((f32[64,1024]{1,0:T(8,128)}), f32[64,1024]{1,0:T(8,128)}) %all-reduce.6.cloned.1.call-update) | async-done | bytes 262160 | tf_op jit(solution)/shard_map/psum | solution.py:56
  177.1 6.5 %fusion = bf16[1,1024,1024]{2,1,0:T(8,128)(2,1)} fusion(f32[64,1024]{1,0:T(8,128)S(1)} %fusion.8, f32[64,1024]{1,0:T(8,128)} %all-reduce.6.cloned.1.call-done, f32[1024,1024]{1,0:T(8,128)} %copy-done.1, bf16[1,1024,1024]{2,1,0:T(8,128)(2,1)S(1)} %copy-done.2), kind=kOutput, calls=%fused_computation.4 | convolution fusion | flops 810549248 | bytes 8912896 | tf_op jit(solution)/shard_map/dot_general | solution.py:60
  183.5 0.7 all-reduce.8.cloned.1.call-update
  184.3 25.5 %all-reduce.8.cloned.1.call-done = f32[64,1024]{1,0:T(8,128)} async-done(((f32[64,1024]{1,0:T(8,128)}), f32[64,1024]{1,0:T(8,128)}) %all-reduce.8.cloned.1.call-update) | async-done | bytes 262160 | tf_op jit(solution)/shard_map/psum | solution.py:57
  209.8 1.1 multiply_reduce_fusion
  210.9 6.0 %psum.47 = f32[64]{0:T(128)S(1)} all-reduce(f32[64]{0:T(128)S(1)} %multiply_reduce_fusion), channel_id=1, replica_groups=mesh['dp'=2,'fsdp'=4,'tensor'=4] {'tensor'}, use_global_device_ids=true, to_apply=%region_9.12 | all-reduce | flops 64 | bytes 512 | tf_op jit(solution)/shard_map/psum | solution.py:58
  216.9 1.0 multiply_divide_fusion
  218.0 6.8 %multiply_subtract_fusion = f32[1024,1024]{1,0:T(8,128)} fusion(f32[1024,1024]{1,0:T(8,128)} %param.7, f32[64,1024]{1,0:T(8,128)S(1)} %fusion.8, f32[64,1024]{1,0:T(8,128)S(1)} %multiply_divide_fusion), kind=kOutput, calls=%fused_computation.3 | convolution fusion | flops 807403520 | bytes 8912896 | tf_op jit(solution)/shard_map/dot_general | solution.py:65
  (22 shorter events, 1.8 us)
Async XLA Ops:
  7.2 6.0 %copy-start = (f32[64,1024]{1,0:T(8,128)S(1)}, f32[64,1024]{1,0:T(8,128)}, u32[]{:S(2)}) copy-start(f32[64,1024]{1,0:T(8,128)} %param.10) | copy-start | bytes 786436
  7.2 6.0 %copy-start.2 = (bf16[1,1024,1024]{2,1,0:T(8,128)(2,1)S(1)}, bf16[1,1024,1024]{2,1,0:T(8,128)(2,1)}, u32[]{:S(2)}) copy-start(bf16[1,1024,1024]{2,1,0:T(8,128)(2,1)} %param.8) | copy-start | bytes 6291460
  7.2 67.9 %all-reduce.4.cloned.1.call-start = ((), (), s32[]{:S(2)}) async-start(), calls=%async_computation | async-start | bytes 524288 | tf_op jit(solution)/shard_map/psum | solution.py:48
  11.2 2.0 copy-start.1
  18.4 158.7 %all-reduce.6.cloned.1.call-start = ((), (), s32[]{:S(2)}) async-start(), calls=%async_computation.1 | async-start | bytes 524288 | tf_op jit(solution)/shard_map/psum | solution.py:56
  183.5 26.3 %all-reduce.8.cloned.1.call-start = ((), (), s32[]{:S(2)}) async-start(), calls=%async_computation.2 | async-start | bytes 524288 | tf_op jit(solution)/shard_map/psum | solution.py:57
  218.0 6.8 %copy-start.3 = (f32[64,1024]{1,0:T(8,128)}, f32[64,1024]{1,0:T(8,128)S(1)}, u32[]{:S(2)}) copy-start(f32[64,1024]{1,0:T(8,128)S(1)} %multiply_divide_fusion) | copy-start | bytes 786436
Sparse Core Ops, SparseCore 0:
  18.5 56.5 all-reduce.3
  144.0 32.9 all-reduce.5
  186.6 23.1 all-reduce.7
where the time goes:
time: 232 us; the launch traced here: 231 us
  waiting for transfers between devices  116 us (50%)
  blocking collectives  41.2 us (18%)
  other arithmetic  30.3 us (13%)
  matrix products  27.7 us (12%)
  between operations  13.9 us (6%)
    psum x1, waiting for transfers between devices, local(): left = orthonormal_rows(lax.psum(partial_value, ('dp', 'tensor')))  56.7 us
    psum x2, blocking collectives, orthonormal_rows(): gram = lax.psum(local_gram(factor), 'fsdp')  35.1 us
    psum x1, waiting for transfers between devices, local(): replica_right = lax.psum(partial_right, 'fsdp')  33.2 us
    psum x1, waiting for transfers between devices, local(): shared = lax.psum(replica_right, 'dp') / replicas  25.5 us
    another operation x6, other arithmetic, cholesky_step(): lower = jnp.linalg.cholesky(gram)  13 us
    another operation x4, other arithmetic, cholesky_step(): return jax.scipy.linalg.solve_triangular(lower, factor.T, lower=True).T  11.1 us
    dot_general x1, matrix products, local(): jnp.dot(left, new_right, precision=lax.Precision.HIGHEST, preferred_eleme...  6.81 us
    dot_general x1, matrix products, local(): jnp.dot(left, replica_right, precision=lax.Precision.HIGHEST, preferred_e...  6.46 us
  transfers between devices with their start and end apart: 3, of which 3 were waited for; matrix products, arithmetic and copies ran while one was open for 0% of the time, Pallas kernels for 0%

commit v1 on v0

--- a/solution.py
+++ b/solution.py
@@ -54,7 +54,7 @@
         preferred_element_type=jnp.float32,
     )
     replica_right = lax.psum(partial_right, "fsdp")
-    shared = lax.psum(replica_right, "dp") / replicas
+    shared = jnp.sum(lax.all_gather(replica_right, "dp"), axis=0) / replicas
     sums = lax.psum(jnp.sum(shared * shared, axis=1), "tensor")
     new_right = normalize(shared, sums)
     projected = jnp.dot(

time: 232 us -> 209 us (0.901)
  waiting for transfers between devices: 116 us -> 89.9 us
  blocking collectives: 41.2 us -> 48 us
    psum x1 -> x0, waiting for transfers between devices: 25.5 us -> none  [local(): shared = lax.psum(replica_right, 'dp') / replicas]
    all_gather x0 -> x1, blocking collectives: none -> 7.24 us  [local(): shared = jnp.sum(lax.all_gather(replica_right, 'dp'), axis=0) / replicas]
  transfers between devices with their start and end apart: 3 -> 2, of which waited for: 3 -> 2; matrix products, arithmetic and copies ran while one was open for 0% -> 0% of each run, Pallas kernels for 0% -> 0%
where the time goes in v1:
time: 209 us
  waiting for transfers between devices  89.9 us (43%)
  blocking collectives  48 us (23%)
  other arithmetic  28.4 us (14%)
  matrix products  26.3 us (13%)
  between operations  14.2 us (7%)
  local copies, waits for them, and re-layouts  2.09 us (1%)
    psum x1, waiting for transfers between devices, local(): left = orthonormal_rows(lax.psum(partial_value, ('dp', 'tensor')))  56.7 us
    psum x2, blocking collectives, orthonormal_rows(): gram = lax.psum(local_gram(factor), 'fsdp')  35.1 us
    psum x1, waiting for transfers between devices, local(): replica_right = lax.psum(partial_right, 'fsdp')  33.2 us
    another operation x6, other arithmetic, cholesky_step(): lower = jnp.linalg.cholesky(gram)  13 us
    another operation x4, other arithmetic, cholesky_step(): return jax.scipy.linalg.solve_triangular(lower, factor.T, lower=True).T  11.1 us
    all_gather x1, blocking collectives, local(): shared = jnp.sum(lax.all_gather(replica_right, 'dp'), axis=0) / replicas  7.24 us
    dot_general x1, matrix products, local(): jnp.dot(left, new_right, precision=lax.Precision.HIGHEST, preferred_eleme...  6.87 us
    dot_general x1, matrix products, local(): lax.dot_general(left, blended, (((0,), (0,)), ((), ())), precision=lax.Pr...  5.74 us
  transfers between devices with their start and end apart: 2, of which 2 were waited for; matrix products, arithmetic and copies ran while one was open for 0% of the time, Pallas kernels for 0%

profile of v1, /device:TPU:0, one launch (start us, length us, event | category | flops | bytes accessed | tf_op | source)
XLA Modules:
  0.0 209.0 jit_solution(10611039918407358169)
XLA Ops:
  7.2 4.0 %convert_reduce_fusion = f32[1024,1024]{1,0:T(8,128)S(1)} fusion(bf16[1,2,1024,1024]{3,2,1,0:T(8,128)(2,1)} %param.9), kind=kLoop, calls=%fused_computation | loop fusion | flops 3145728 | bytes 8388608 | tf_op jit(solution)/shard_map/reduce_sum | solution.py:38
  11.2 1.9 copy-done.1
  13.1 5.1 %fusion.3 = f32[1024,64]{0,1:T(8,128)} fusion(f32[64,1024]{1,0:T(8,128)S(1)} %copy-done, f32[1024,1024]{1,0:T(8,128)S(1)} %convert_reduce_fusion, bf16[1,1024,1024]{2,1,0:T(8,128)(2,1)S(1)} %copy-done.3), kind=kOutput, calls=%fused_computation.7 | convolution fusion | flops 807469056 | bytes 6815744 | tf_op jit(solution)/shard_map/dot_general | solution.py:40
  18.3 56.7 %all-reduce.3.cloned.1.call-done = f32[1024,64]{0,1:T(8,128)} async-done(((f32[1024,64]{0,1:T(8,128)}), f32[1024,64]{0,1:T(8,128)}) %all-reduce.3.cloned.1.call-update) | async-done | bytes 262160 | tf_op jit(solution)/shard_map/psum | solution.py:48
  75.0 1.4 fusion.15
  76.4 19.0 %psum.36 = f32[64,64]{0,1:T(8,128)S(1)} all-reduce(f32[64,64]{0,1:T(8,128)S(1)} %fusion.15), channel_id=1, replica_groups=mesh['dp'=2,'fsdp'=4,'tensor'=4] {'fsdp'}, use_global_device_ids=true, to_apply=%region_2.0 | all-reduce | flops 4096 | bytes 32768 | tf_op jit(solution)/shard_map/psum | solution.py:27
  95.5 5.8 %cholesky.44 = f32[64,64]{1,0:T(8,128)S(1)} custom-call(f32[64,64]{1,0:T(8,128)S(1)} %fusion.12), custom_call_target="Cholesky" | custom-call | tf_op jit(solution)/shard_map/jit(cholesky)/cholesky | solution.py:15
  101.4 0.6 compare_reduce_fusion.1
  102.0 0.7 fusion.6
  102.7 4.9 %custom-call.6 = f32[1,64,64]{1,2,0:T(8,128)S(1)} custom-call(f32[1,64,64]{2,1,0:T(8,128)S(1)} %fusion.6), custom_call_target="InvertDiagBlocksLowerTriangular" | custom-call | tf_op jit(solution)/shard_map/jit(_solve_triangular)/triangular_solve | solution.py:16
  107.6 1.4 fusion.4
  109.0 0.4 fusion.16
  109.3 16.1 %psum.37 = f32[64,64]{0,1:T(8,128)S(1)} all-reduce(f32[64,64]{0,1:T(8,128)S(1)} %fusion.16), channel_id=1, replica_groups=mesh['dp'=2,'fsdp'=4,'tensor'=4] {'fsdp'}, use_global_device_ids=true, to_apply=%region_5.0 | all-reduce | flops 4096 | bytes 32768 | tf_op jit(solution)/shard_map/psum | solution.py:27
  125.6 5.8 %cholesky.55 = f32[64,64]{1,0:T(8,128)S(1)} custom-call(f32[64,64]{1,0:T(8,128)S(1)} %fusion.10), custom_call_target="Cholesky" | custom-call | tf_op jit(solution)/shard_map/jit(cholesky)/cholesky | solution.py:15
  131.5 0.6 compare_reduce_fusion
  132.1 0.7 fusion.7
  132.8 4.9 %custom-call.7 = f32[1,64,64]{1,2,0:T(8,128)S(1)} custom-call(f32[1,64,64]{2,1,0:T(8,128)S(1)} %fusion.7), custom_call_target="InvertDiagBlocksLowerTriangular" | custom-call | tf_op jit(solution)/shard_map/jit(_solve_triangular)/triangular_solve | solution.py:16
  137.7 0.4 fusion.8
  138.1 5.7 %fusion.1 = f32[64,1024]{1,0:T(8,128)} fusion(f32[64,1024]{1,0:T(8,128)S(1)} %fusion.8, f32[1024,1024]{1,0:T(8,128)} %copy-done.1, bf16[1,1024,1024]{2,1,0:T(8,128)(2,1)S(1)} %copy-done.3), kind=kOutput, calls=%fused_computation.5 | convolution fusion | flops 807403520 | bytes 6815744 | tf_op jit(solution)/shard_map/dot_general | solution.py:49
  143.9 33.2 %all-reduce.5.cloned.1.call-done = f32[64,1024]{1,0:T(8,128)} async-done(((f32[64,1024]{1,0:T(8,128)}), f32[64,1024]{1,0:T(8,128)}) %all-reduce.5.cloned.1.call-update) | async-done | bytes 262160 | tf_op jit(solution)/shard_map/psum | solution.py:56
  177.0 7.2 %all-gather = f32[128,1024]{1,0:T(8,128)S(1)} all-gather(f32[64,1024]{1,0:T(8,128)} %all-reduce.5.cloned.1.call-done), channel_id=2, replica_groups=mesh['dp'=2,'fsdp'=4,'tensor'=4] {'dp'}, dimensions={0}, use_global_device_ids=true | all-gather | bytes 786432 | tf_op jit(solution)/shard_map/all_gather | solution.py:57
  184.4 5.7 %psum.39 = f32[64]{0:T(128)S(1)} all-reduce(f32[64]{0:T(128)S(1)} %multiply_reduce_fusion), channel_id=1, replica_groups=mesh['dp'=2,'fsdp'=4,'tensor'=4] {'tensor'}, use_global_device_ids=true, to_apply=%region_9.12 | all-reduce | flops 64 | bytes 512 | tf_op jit(solution)/shard_map/psum | solution.py:58
  190.2 6.9 %multiply_subtract_fusion = f32[1024,1024]{1,0:T(8,128)} fusion(f32[1024,1024]{1,0:T(8,128)} %param.7, f32[64,1024]{1,0:T(8,128)S(1)} %fusion.8, f32[64,1024]{1,0:T(8,128)S(1)} %multiply_divide_fusion), kind=kOutput, calls=%fused_computation.3 | convolution fusion | flops 807403520 | bytes 8912896 | tf_op jit(solution)/shard_map/dot_general | solution.py:65
  197.1 5.1 %fusion = bf16[1,1024,1024]{2,1,0:T(8,128)(2,1)} fusion(f32[64,1024]{1,0:T(8,128)S(1)} %fusion.8, f32[64,1024]{1,0:T(8,128)S(1)} %copy-done.4, f32[1024,1024]{1,0:T(8,128)S(1)} %copy-done.2, bf16[1,1024,1024]{2,1,0:T(8,128)(2,1)S(1)} %copy-done.3), kind=kOutput, calls=%fused_computation.4 | convolution fusion | flops 810549248 | bytes 8912896 | tf_op jit(solution)/shard_map/dot_general | solution.py:60
  (25 shorter events, 0.6 us)
Async XLA Ops:
  7.2 6.0 %copy-start = (f32[64,1024]{1,0:T(8,128)S(1)}, f32[64,1024]{1,0:T(8,128)}, u32[]{:S(2)}) copy-start(f32[64,1024]{1,0:T(8,128)} %param.10) | copy-start | bytes 786436
  7.2 5.9 %copy-start.3 = (bf16[1,1024,1024]{2,1,0:T(8,128)(2,1)S(1)}, bf16[1,1024,1024]{2,1,0:T(8,128)(2,1)}, u32[]{:S(2)}) copy-start(bf16[1,1024,1024]{2,1,0:T(8,128)(2,1)} %param.8) | copy-start | bytes 6291460
  7.2 67.8 %all-reduce.3.cloned.1.call-start = ((), (), s32[]{:S(2)}) async-start(), calls=%async_computation | async-start | bytes 524288 | tf_op jit(solution)/shard_map/psum | solution.py:48
  11.2 1.9 copy-start.1
  18.3 158.7 %all-reduce.5.cloned.1.call-start = ((), (), s32[]{:S(2)}) async-start(), calls=%async_computation.1 | async-start | bytes 524288 | tf_op jit(solution)/shard_map/psum | solution.py:56
  190.2 6.9 %copy-start.5 = (f32[64,1024]{1,0:T(8,128)}, f32[64,1024]{1,0:T(8,128)S(1)}, u32[]{:S(2)}) copy-start(f32[64,1024]{1,0:T(8,128)S(1)} %multiply_divide_fusion) | copy-start | bytes 786436
  190.2 6.9 %copy-start.2 = (f32[1024,1024]{1,0:T(8,128)S(1)}, f32[1024,1024]{1,0:T(8,128)}, u32[]{:S(2)}) copy-start(f32[1024,1024]{1,0:T(8,128)} %copy-done.1) | copy-start | bytes 12582916
  190.2 6.9 %copy-start.4 = (f32[64,1024]{1,0:T(8,128)S(1)}, f32[64,1024]{1,0:T(8,128)}, u32[]{:S(2)}) copy-start(f32[64,1024]{1,0:T(8,128)} %all-reduce.5.cloned.1.call-done) | copy-start | bytes 786436
Sparse Core Ops, SparseCore 0:
  18.4 56.5 all-reduce.2
  144.0 32.9 all-reduce.4
